TPU v7x, 1024 devices: a whole 4x8x16 slice. The times are simulated.
1024 devices in a mesh: wide: 64 (over x, y, core), narrow: 16 (over z).
Axes of the slice: x: 4, y: 8, z: 16, core: 2. Of those that a mesh axis runs over, the one named last changes fastest.
Arguments:
- amplitudes: bfloat16 [8192, 1024], P('narrow'), may hold values from -6 to 6
- integrals: bfloat16 [4096, 128, 128], P('wide', 'narrow'), may hold values from -0.5 to 0.5
- in_tile: int32 [4096], P('wide'), may hold values from 0 to 7
- counts: int32 [64], P('wide'), may hold values from 1 to 64, as said below
- out_tile: int32 [4096], P('wide'), may hold values from 0 to 127, as said below
- owner_map: int32 [128], replicated, may hold values from 0 to 127, as said below
Outputs:
- residual: float32 [8192, 16384], P('narrow', 'wide')
Inputs may be any that keep to these rules, and one draw needn't show every extreme that they name: `counts`: some home device has exactly 64 live tasks in every draw. `out_tile`: call device owner_map[t] // 2 the owner of tile t. The 64 slots of one home device have tiles of pairwise different owners, and the live tasks of all homes give one owner at most 32 tasks; some owner receives exactly 32 in every draw. `owner_map`: A permutation of the residual tiles.
All inputs are finite; a program needn't handle non-finite values.
Results may differ from a plain program's by a relative error of at most 0.0029.
Values may be sent and summed in bfloat16 or wider, within the bound.
A program may use at most 32 MiB of HBM per device.

v0:
```python
import jax
import jax.numpy as jnp
from jax import lax
from jax.sharding import PartitionSpec as P


def tile_position(tile_ids, owner_map):
    tile_total = owner_map.shape[0]
    hit = tile_ids[:, None] == jnp.arange(tile_total, dtype=jnp.int32)[None, :]
    return jnp.sum(jnp.where(hit, owner_map[None, :], 0), axis=1)


def shards(amplitudes, integrals, in_tile, counts, out_tile, owner_map):
    slot_count = integrals.shape[0]
    tile_width = integrals.shape[2]
    recv_count = slot_count // 2
    row_count = amplitudes.shape[0]
    tile_count = amplitudes.shape[1] // tile_width
    wide_count = lax.axis_size("wide")
    own_count = owner_map.shape[0] // wide_count
    slot_ids = jnp.arange(slot_count, dtype=jnp.int32)
    is_live = slot_ids < counts[0]
    target = tile_position(out_tile, owner_map) // own_count
    task_label = jnp.where(is_live, out_tile + 1, 0)
    task_meta = jnp.stack([task_label, in_tile], 1).astype(jnp.float32)
    owners = jnp.arange(wide_count, dtype=jnp.int32)[:, None]
    send_match = is_live[None, :] & (target[None, :] == owners)
    send_meta = jnp.dot(send_match.astype(jnp.float32), task_meta).astype(jnp.bfloat16)
    full = lax.all_gather(integrals, "narrow", axis=1, tiled=True)
    send_rows = jnp.einsum(
        "oh,hrc->orc", send_match.astype(jnp.bfloat16), full, preferred_element_type=jnp.float32
    ).astype(jnp.bfloat16)
    pieces, task_info = (
        lax.all_to_all(send_rows, "wide", split_axis=0, concat_axis=0, tiled=True),
        lax.all_to_all(send_meta, "wide", split_axis=0, concat_axis=0, tiled=True),
    )
    task_info = task_info.astype(jnp.float32)
    is_mine = task_info[:, 0] > 0.5
    compact_rank = jnp.cumsum(is_mine.astype(jnp.int32)) - 1
    pick_rows = (
        is_mine[None, :]
        & (compact_rank[None, :] == jnp.arange(recv_count, dtype=jnp.int32)[:, None])
    ).astype(jnp.bfloat16)
    chosen = jnp.einsum(
        "um,mrc->urc", pick_rows, pieces, preferred_element_type=jnp.float32
    ).astype(jnp.bfloat16)
    chosen_info = jnp.dot(pick_rows.astype(jnp.float32), task_info)
    tile_ids = chosen_info[:, 0].astype(jnp.int32) - 1
    source_tile = chosen_info[:, 1].astype(jnp.int32)
    blocks = amplitudes.reshape(row_count, tile_count, tile_width)
    pick_in = (source_tile[:, None] == jnp.arange(tile_count, dtype=jnp.int32)[None, :]).astype(
        jnp.bfloat16
    )
    selected = jnp.einsum(
        "uk,pkc->upc", pick_in, blocks, preferred_element_type=jnp.float32
    ).astype(jnp.bfloat16)
    products = jnp.einsum(
        "upr,urc->upc", selected, chosen, preferred_element_type=jnp.float32
    ).astype(jnp.bfloat16)
    local_place = tile_position(tile_ids, owner_map) % own_count
    assign_out = (
        (tile_ids[:, None] >= 0)
        & (local_place[:, None] == jnp.arange(own_count, dtype=jnp.int32)[None, :])
    ).astype(jnp.bfloat16)
    result = jnp.einsum("uj,upc->pjc", assign_out, products, preferred_element_type=jnp.float32)
    return result.reshape(row_count, own_count * tile_width)


def solution(mesh):
    return jax.shard_map(
        shards,
        mesh=mesh,
        in_specs=(
            P("narrow", None),
            P("wide", "narrow", None),
            P("wide"),
            P("wide"),
            P("wide"),
            P(),
        ),
        out_specs=P("narrow", "wide"),
        check_vma=False,
    )
```

profile of v0, /device:TPU:1, one launch (start us, length us, event | category | flops | bytes accessed | tf_op | source)
XLA Modules:
  0.0 178.1 jit_solution(12745109179733301459)
XLA Ops:
  6.5 0.0 all-gather.2.cloned.1.call-start
  6.5 1.6 copy.28
  8.1 0.0 all-gather.2.cloned.1.call-update
  8.8 0.8 select_reduce_fusion
  9.7 0.7 select_bitcast_fusion
  10.3 0.8 fusion.12
  11.1 0.7 copy.25
  11.8 18.1 %all-to-all-start = ((bf16[64,1,2]{2,1,0:T(2,128)(2,1)}), bf16[64,1,2]{2,1,0:T(2,128)(2,1)S(1)}, u32[]{:S(2)}, u32[]{:S(2)}) async-start(bf16[64,1,2]{2,1,0:T(2,128)(2,1)} %copy.25), calls=%async_computation | async-start | bytes 65536 | tf_op jit(solution)/shard_map/all_to_all | solution.py:35
  29.9 55.9 %all-gather.2.cloned.1.call-done = bf16[64,128,128]{2,0,1:T(8,128)(2,1)} async-done(((bf16[64,8,128]{2,0,1:T(8,128)(2,1)}), bf16[64,128,128]{2,0,1:T(8,128)(2,1)}) %all-gather.2.cloned.1.call-update) | async-done | bytes 2097168 | tf_op jit(solution)/shard_map/all_gather | solution.py:29
  85.9 2.3 %convolution_convert_fusion.1 = bf16[64,128,128]{2,0,1:T(8,128)(2,1)S(1)} fusion(bf16[64,128,128]{2,0,1:T(8,128)(2,1)} %all-gather.2.cloned.1.call-done, s32[64]{0:T(128)S(1)} %and_select_fusion.1, pred[64]{0:T(512)(128)(4,1)S(1)} %iota_compare_fusion.5), kind=kOutput, calls=%fused_computation.8 | convolution fusion | flops 135274496 | bytes 4194624 | tf_op jit(solution)/shard_map/oh,hrc->orc/dot_general | solution.py:30
  88.2 2.7 %copy.29 = bf16[64,128,128]{2,1,0:T(8,128)(2,1)} copy(bf16[64,128,128]{2,0,1:T(8,128)(2,1)S(1)} %convolution_convert_fusion.1) | data formatting | bytes 4194304 | tf_op jit(solution)/shard_map/convert_element_type | solution.py:32
  90.8 0.0 copy-start
  90.8 0.0 all-to-all-done
  90.8 20.0 %all-to-all-start.1 = ((bf16[64,128,128]{2,1,0:T(8,128)(2,1)}), bf16[64,128,128]{2,1,0:T(8,128)(2,1)S(1)}, u32[]{:S(2)}, u32[]{:S(2)}) async-start(bf16[64,128,128]{2,1,0:T(8,128)(2,1)} %copy.29), calls=%async_computation.1 | async-start | bytes 4194304 | tf_op jit(solution)/shard_map/all_to_all | solution.py:34
  110.8 1.5 copy.34
  112.3 0.1 copy.26
  112.4 0.1 copy.27
  112.5 0.1 reduce-window.8
  112.6 0.1 add_reduce_fusion
  112.8 0.1 fusion.22
  112.9 0.0 copy-done
  112.9 0.2 select_reduce_fusion.1
  113.1 3.2 %convolution_convert_fusion = bf16[32,512,128]{2,0,1:T(8,128)(2,1)} fusion(bf16[512,8,128]{2,1,0:T(8,128)(2,1)S(1)} %bitcast.40, s32[32]{0:T(128)S(1)} %convert_bitcast_fusion), kind=kOutput, calls=%fused_computation.4 | convolution fusion | flops 35651840 | bytes 5243008 | tf_op jit(solution)/shard_map/uk,pkc->upc/dot_general | solution.py:54
  116.3 45.7 %all-to-all-done.1 = bf16[64,128,128]{2,1,0:T(8,128)(2,1)S(1)} async-done(((bf16[64,128,128]{2,1,0:T(8,128)(2,1)}), bf16[64,128,128]{2,1,0:T(8,128)(2,1)S(1)}, u32[]{:S(2)}, u32[]{:S(2)}) %all-to-all-start.1) | async-done | bytes 2097184 | tf_op jit(solution)/shard_map/all_to_all | solution.py:34
  162.0 1.5 fusion.9
  163.6 4.4 %fusion.4 = bf16[32,512,128]{2,1,0:T(8,128)(2,1)S(1)} fusion(bf16[32,512,128]{2,0,1:T(8,128)(2,1)} %convolution_convert_fusion, bf16[32,128,128]{2,0,1:T(8,128)(2,1)S(1)} %fusion.9), kind=kOutput, calls=%fused_computation.5 | convolution fusion | flops 538968064 | bytes 9437184 | tf_op jit(solution)/shard_map/upr,urc->upc/dot_general | solution.py:57
  168.0 2.4 %fusion = f32[512,128,2]{1,2,0:T(2,128)S(1)} fusion(bf16[32,512,128]{2,1,0:T(8,128)(2,1)S(1)} %fusion.4, pred[32]{0:T(512)(128)(4,1)S(1)} %compare_bitcast_fusion, s32[32]{0:T(128)S(1)} %and_select_fusion), kind=kOutput, calls=%fused_computation | convolution fusion | flops 8388736 | bytes 4718752 | tf_op jit(solution)/shard_map/uj,upc->pjc/dot_general | solution.py:65
  170.4 0.8 copy.49
  (7 shorter events, 0.1 us)
Async XLA Ops:
  6.5 79.3 %all-gather.2.cloned.1.call-start = ((), (), s32[]{:S(2)}) async-start(), calls=%async_computation.2 | async-start | bytes 2228224 | tf_op jit(solution)/shard_map/all_gather | solution.py:29
  11.8 79.0 %all-to-all-start = ((bf16[64,1,2]{2,1,0:T(2,128)(2,1)}), bf16[64,1,2]{2,1,0:T(2,128)(2,1)S(1)}, u32[]{:S(2)}, u32[]{:S(2)}) async-start(bf16[64,1,2]{2,1,0:T(2,128)(2,1)} %copy.25), calls=%async_computation | async-start | bytes 65536 | tf_op jit(solution)/shard_map/all_to_all | solution.py:35
  90.8 22.1 %copy-start = (s32[128]{0:T(128)S(1)}, s32[128]{0:T(128)}, u32[]{:S(2)}) copy-start(s32[128]{0:T(128)} %param.11) | copy-start | bytes 1540
  90.8 71.2 %all-to-all-start.1 = ((bf16[64,128,128]{2,1,0:T(8,128)(2,1)}), bf16[64,128,128]{2,1,0:T(8,128)(2,1)S(1)}, u32[]{:S(2)}, u32[]{:S(2)}) async-start(bf16[64,128,128]{2,1,0:T(8,128)(2,1)} %copy.29), calls=%async_computation.1 | async-start | bytes 4194304 | tf_op jit(solution)/shard_map/all_to_all | solution.py:34
Sparse Core Ops, SparseCore 0:
  10.0 75.8 all-gather.1
where the time goes:
time: 178 us
  waiting for transfers between devices  102 us (57%)
  starting transfers between devices  38.1 us (21%)
  matrix products  14.7 us (8%)
  between operations  14.1 us (8%)
  local copies, waits for them, and re-layouts  7.5 us (4%)
  other arithmetic  1.97 us (1%)
    all_gather x1, waiting for transfers between devices, shards(): full = lax.all_gather(integrals, 'narrow', axis=1, tiled=True)  55.9 us
    all_to_all x1, waiting for transfers between devices, shards(): lax.all_to_all(send_rows, 'wide', split_axis=0, concat_axis=0, tiled=True)  45.7 us
    all_to_all x1, starting transfers between devices, shards(): lax.all_to_all(send_rows, 'wide', split_axis=0, concat_axis=0, tiled=True)  20 us
    all_to_all x1, starting transfers between devices, shards(): lax.all_to_all(send_meta, 'wide', split_axis=0, concat_axis=0, tiled=True)  18.1 us
    dot_general x1, matrix products, shards(): jnp.einsum('upr,urc->upc', selected, chosen, preferred_element_type=jnp.f...  4.41 us
    unnamed x5, local copies, waits for them, and re-layouts  3.9 us
  transfers between devices with their start and end apart: 3, of which 2 were waited for; matrix products, arithmetic and copies ran while one was open for 8% of the time, Pallas kernels for 0%

commit v1 on v0

v1 whole, which is shorter than its diff:
```python
import jax
import jax.numpy as jnp
from jax import lax
from jax.sharding import PartitionSpec as P


def shards(amplitudes, integrals, in_tile, counts, out_tile, owner_map):
    slot_count, piece, width = integrals.shape
    tile_total = owner_map.shape[0]
    tile_count = amplitudes.shape[1] // width
    wide_count = lax.axis_size("wide")
    narrow_count = lax.axis_size("narrow")
    own_count = tile_total // wide_count
    bins = own_count * tile_count
    slot_ids = jnp.arange(slot_count, dtype=jnp.int32)
    is_live = slot_ids < counts[0]
    hit = out_tile[:, None] == jnp.arange(tile_total, dtype=jnp.int32)[None, :]
    place = jnp.sum(jnp.where(hit, owner_map[None, :], 0), axis=1)
    label = (place % own_count) * tile_count + in_tile + 1
    target = jnp.where(is_live, place // own_count, -1)
    owners = jnp.arange(wide_count, dtype=jnp.int32)[:, None]
    send_match = (target[None, :] == owners).astype(jnp.bfloat16)
    rows = jnp.concatenate(
        [
            integrals.reshape(slot_count, piece * width),
            jnp.broadcast_to(label[:, None], (slot_count, width)).astype(jnp.bfloat16),
        ],
        axis=1,
    )
    send = jnp.dot(send_match, rows, preferred_element_type=jnp.float32).astype(jnp.bfloat16)
    got = lax.all_to_all(send, "wide", split_axis=0, concat_axis=0, tiled=True)
    got_label = got[:, piece * width].astype(jnp.int32) - 1
    pick = (jnp.arange(bins, dtype=jnp.int32)[:, None] == got_label[None, :]).astype(jnp.bfloat16)
    summed = jnp.dot(
        pick, got[:, : piece * width], preferred_element_type=jnp.float32
    ).astype(jnp.bfloat16)
    summed = summed.reshape(own_count, tile_count, piece, width)
    full = lax.all_gather(summed, "narrow", axis=0)
    full = full.transpose(2, 0, 3, 1, 4)
    full = full.reshape(tile_count, narrow_count * piece, own_count * width)
    full = full.reshape(tile_count * narrow_count * piece, own_count * width)
    return jnp.dot(amplitudes, full, preferred_element_type=jnp.float32)


def solution(mesh):
    return jax.shard_map(
        shards,
        mesh=mesh,
        in_specs=(
            P("narrow", None),
            P("wide", "narrow", None),
            P("wide"),
            P("wide"),
            P("wide"),
            P(),
        ),
        out_specs=P("narrow", "wide"),
        check_vma=False,
    )
```

time: 178 us -> 72.8 us (0.41)
  the two profiles are of different devices: /device:TPU:1 before, /device:TPU:8 now
where the time goes in v1:
time: 72.8 us; the launch traced here: 72.6 us
  blocking collectives  66.3 us (91%)
  local copies, waits for them, and re-layouts  3.65 us (5%)
  other arithmetic  0.98 us (1%)
  between operations  0.84 us (1%)
  matrix products  0.79 us (1%)
    all_gather x1, blocking collectives, shards(): full = lax.all_gather(summed, 'narrow', axis=0)  39.5 us
    all_to_all x1, blocking collectives, shards(): got = lax.all_to_all(send, 'wide', split_axis=0, concat_axis=0, tiled=True)  26.9 us
    unnamed x12, local copies, waits for them, and re-layouts  2.05 us

profile of v1, /device:TPU:8, one launch (start us, length us, event | category | flops | bytes accessed | tf_op | source)
XLA Modules:
  0.0 72.6 jit_solution(4360778430463975572)
XLA Ops:
  0.0 0.0 copy-start
  0.7 0.0 copy-start.2
  0.8 0.0 copy-start.3
  0.8 0.9 %copy.24 = bf16[8,8,8,128]{3,1,2,0:T(8,128)(2,1)S(1)} copy(bf16[8,8,8,128]{3,2,1,0:T(8,128)(2,1)} %bitcast.24) | data formatting | bytes 262144
  1.7 0.0 copy-done.2
  1.7 0.0 copy-done.3
  1.7 0.2 select_reduce_fusion
  1.9 0.0 copy-start.1
  1.9 0.7 copy-done.1
  2.6 0.1 broadcast_in_dim.18
  2.7 0.2 fusion
  2.8 0.5 broadcast.77
  3.4 0.7 reduce.2
  4.0 0.2 reshape.41
  4.2 26.9 %all_to_all.12 = bf16[64,2,576]{2,1,0:T(2,128)(2,1)S(1)} all-to-all(bf16[64,2,576]{2,1,0:T(2,128)(2,1)S(1)} %reshape.41), channel_id=1, replica_groups=mesh['wide'=64,'narrow'=16] {'wide'}, dimensions={0} | all-to-all | bytes 294912 | tf_op jit(solution)/shard_map/all_to_all | solution.py:31
  31.1 0.2 reshape.42
  31.4 0.1 add_reduce_fusion
  31.5 0.1 fusion.1
  31.6 39.5 %all_gather.3 = bf16[16,2,8,8,128]{4,3,1,0,2:T(8,128)(2,1)S(1)} all-gather(bf16[1,2,8,8,128]{4,3,1,0,2:T(8,128)(2,1)S(1)} %copy.17), channel_id=1, replica_groups=mesh['wide'=64,'narrow'=16] {'narrow'}, dimensions={0}, use_global_device_ids=true | all-gather | bytes 557056 | tf_op jit(solution)/shard_map/all_gather | solution.py:38
  71.1 0.0 copy-done
  71.1 0.5 convolution_bitcast_fusion
  71.6 1.0 %copy.18 = f32[512,256]{1,0:T(8,128)} copy(f32[512,256]{0,1:T(8,128)S(1)} %convolution_bitcast_fusion) | data formatting | bytes 1048576 | tf_op jit(solution)/shard_map/dot_general | solution.py:42
  (3 shorter events, 0.0 us)
Async XLA Ops:
  0.0 71.1 %copy-start = (bf16[512,1024]{1,0:T(8,128)(2,1)S(1)}, bf16[512,1024]{1,0:T(8,128)(2,1)}, u32[]{:S(2)}) copy-start(bf16[512,1024]{1,0:T(8,128)(2,1)} %param.6) | copy-start | bytes 3145732
  0.7 1.0 %copy-start.2 = (s32[128]{0:T(128)S(1)}, s32[128]{0:T(128)}, u32[]{:S(2)}) copy-start(s32[128]{0:T(128)} %param.11) | copy-start | bytes 1540
  0.8 1.0 %copy-start.3 = (s32[64]{0:T(128)S(1)}, s32[64]{0:T(128)}, u32[]{:S(2)}) copy-start(s32[64]{0:T(128)} %param.10) | copy-start | bytes 772
  1.9 0.7 copy-start.1

commit v2 on v1

v2 whole, which is shorter than its diff:
```python
import functools

import jax
import jax.numpy as jnp
from jax import lax
from jax.experimental import pallas as pl
from jax.experimental.pallas import tpu as pltpu
from jax.sharding import PartitionSpec as P

MESH = pl.DeviceIdType.MESH
CORES = 2
LABELS = 32


def far_first(count):
    return sorted(range(1, count), key=lambda d: -min(d, count - d))


def exchange(
    sizes,
    code_ref,
    tiles_ref,
    full_ref,
    send,
    send_label,
    mid,
    mid_label,
    got,
    got_label,
    y_send,
    y_recv,
    yl_send,
    yl_recv,
    e_send,
    e_recv,
    el_send,
    el_recv,
    up_send,
    up_recv,
    down_send,
    down_recv,
):
    x_count, y_count, own_count, tile_count = sizes
    e_count = x_count * CORES
    width = tiles_ref.shape[2]
    n_count = lax.axis_size("narrow")
    wide = lax.axis_index("wide")
    me = lax.axis_index("narrow")
    core = wide % CORES
    y = (wide // CORES) % y_count
    x = wide // (CORES * y_count)

    def wide_at(dy, de):
        to_x = (x + de // CORES) % x_count
        to_y = (y + dy) % y_count
        to_core = (core + de % CORES) % CORES
        return (to_x * y_count + to_y) * CORES + to_core

    up, down = (me + 1) % n_count, (me + n_count - 1) % n_count
    y_order = far_first(y_count)
    e_order = sorted(range(1, e_count), key=lambda d: -min(d // CORES, x_count - d // CORES))

    barrier = pltpu.get_barrier_semaphore()
    for dy in y_order:
        pl.semaphore_signal(barrier, inc=1, device_id={"wide": wide_at(dy, 0)}, device_id_type=MESH)
    for de in e_order:
        pl.semaphore_signal(barrier, inc=1, device_id={"wide": wide_at(0, de)}, device_id_type=MESH)
    pl.semaphore_signal(barrier, inc=1, device_id={"narrow": up}, device_id_type=MESH)
    pl.semaphore_signal(barrier, inc=1, device_id={"narrow": down}, device_id_type=MESH)

    for dy in y_order + [0]:
        rows, labels = (send.at[dy], send_label.at[dy]) if dy else (mid.at[0], mid_label.at[0])
        for de in range(e_count):
            code = code_ref[wide_at(dy, de)]
            rows[de] = tiles_ref[code // LABELS]
            labels[de] = jnp.full((1, width), code % LABELS, jnp.int32).astype(jnp.float32)

    pl.semaphore_wait(barrier, y_count + e_count)

    started = []

    def start(src, dst, send_sem, recv_sem, device):
        copy = pltpu.make_async_remote_copy(
            src_ref=src,
            dst_ref=dst,
            send_sem=send_sem,
            recv_sem=recv_sem,
            device_id=device,
            device_id_type=MESH,
        )
        copy.start()
        started.append(copy)
        return copy

    first = []
    for dy in y_order:
        to = {"wide": wide_at(dy, 0)}
        first.append(start(send_label.at[dy], mid_label.at[dy], yl_send.at[dy], yl_recv.at[dy], to))
        first.append(start(send.at[dy], mid.at[dy], y_send.at[dy], y_recv.at[dy], to))
    for copy in first:
        copy.wait_recv()
    second = {}
    for de in e_order:
        to = {"wide": wide_at(0, de)}
        second[de] = (
            start(mid_label.at[:, de], got_label.at[de], el_send.at[de], el_recv.at[de], to),
            start(mid.at[:, de], got.at[de], e_send.at[de], e_recv.at[de], to),
        )

    bins = own_count * tile_count
    sums = [jnp.zeros(tiles_ref.shape[1:], jnp.float32) for _ in range(bins)]
    for de in [0] + e_order[::-1]:
        for copy in second.get(de, ()):
            copy.wait_recv()
        for j in range(y_count):
            tile = (got[de, j] if de else mid[j, 0]).astype(jnp.float32)
            label = got_label[de, j] if de else mid_label[j, 0]
            label = jnp.broadcast_to(label, tile.shape)
            for b in range(bins):
                sums[b] = sums[b] + jnp.where(label == float(b + 1), tile, 0.0)
    for q in range(own_count):
        for k in range(tile_count):
            full_ref[k, me, :, q * width : (q + 1) * width] = sums[q * tile_count + k].astype(
                jnp.bfloat16
            )

    up_steps, down_steps = n_count // 2, (n_count - 1) // 2
    ups, downs = [], []
    for step in range(up_steps):
        if step:
            ups[-1].wait_recv()
        block = full_ref.at[:, (me + n_count - step) % n_count]
        ups.append(start(block, block, up_send.at[step], up_recv.at[step], {"narrow": up}))
        if step < down_steps:
            if step:
                downs[-1].wait_recv()
            block = full_ref.at[:, (me + step) % n_count]
            downs.append(
                start(block, block, down_send.at[step], down_recv.at[step], {"narrow": down})
            )
    ups[-1].wait_recv()
    if downs:
        downs[-1].wait_recv()
    for copy in started:
        copy.wait_send()


def shards(x_count, y_count, amplitudes, integrals, in_tile, counts, out_tile, owner_map):
    slot_count, piece, width = integrals.shape
    tile_total = owner_map.shape[0]
    wide_count = lax.axis_size("wide")
    narrow_count = lax.axis_size("narrow")
    tile_count = amplitudes.shape[1] // (piece * narrow_count)
    own_count = tile_total // wide_count
    e_count = x_count * CORES
    slot_ids = jnp.arange(slot_count, dtype=jnp.int32)
    hit = out_tile[:, None] == jnp.arange(tile_total, dtype=jnp.int32)[None, :]
    place = jnp.sum(jnp.where(hit, owner_map[None, :], 0), axis=1)
    label = (place % own_count) * tile_count + in_tile + 1
    target = jnp.where(slot_ids < counts[0], place // own_count, -1)
    owners = jnp.arange(wide_count, dtype=jnp.int32)[:, None]
    slot_code = slot_ids * LABELS + label
    code = jnp.sum(jnp.where(target[None, :] == owners, slot_code[None, :], 0), axis=1)
    rows = pltpu.VMEM
    dma = pltpu.SemaphoreType.DMA
    bf16, f32 = jnp.bfloat16, jnp.float32
    full = pl.pallas_call(
        functools.partial(exchange, (x_count, y_count, own_count, tile_count)),
        out_shape=jax.ShapeDtypeStruct((tile_count, narrow_count, piece, own_count * width), bf16),
        in_specs=[
            pl.BlockSpec(memory_space=pltpu.SMEM),
            pl.BlockSpec(memory_space=pltpu.VMEM),
        ],
        out_specs=pl.BlockSpec(memory_space=pltpu.VMEM),
        scratch_shapes=[
            rows((y_count, e_count, piece, width), bf16),
            rows((y_count, e_count, 1, width), f32),
            rows((y_count, e_count, piece, width), bf16),
            rows((y_count, e_count, 1, width), f32),
            rows((e_count, y_count, piece, width), bf16),
            rows((e_count, y_count, 1, width), f32),
        ]
        + [dma((y_count,))] * 4
        + [dma((e_count,))] * 4
        + [dma((narrow_count,))] * 4,
        compiler_params=pltpu.CompilerParams(collective_id=0, has_side_effects=True),
    )(code, integrals)
    full = full.reshape(tile_count * narrow_count * piece, own_count * width)
    return jnp.dot(amplitudes, full, preferred_element_type=jnp.float32)


def solution(mesh):
    wide_count = mesh.shape["wide"]
    y_count = 8 if wide_count == 64 else 2
    x_count = wide_count // (CORES * y_count)
    return jax.shard_map(
        functools.partial(shards, x_count, y_count),
        mesh=mesh,
        in_specs=(
            P("narrow", None),
            P("wide", "narrow", None),
            P("wide"),
            P("wide"),
            P("wide"),
            P(),
        ),
        out_specs=P("narrow", "wide"),
        check_vma=False,
    )
```

time: 72.8 us -> 61.2 us (0.84)
  blocking collectives: 66.3 us -> 0 us
  Pallas kernels: 0 us -> 55.7 us
  local copies, waits for them, and re-layouts: 3.65 us -> 2.14 us
  matrix products: 0.79 us -> 1.52 us
    pallas_call x0 -> x1, Pallas kernels: none -> 55.7 us  [shards(): pl.pallas_call(functools.partial(exchange, (x_count, y_count, own_count,...]
    all_gather x1 -> x0, blocking collectives: 39.5 us -> none  [shards(): full = lax.all_gather(summed, 'narrow', axis=0)]
    all_to_all x1 -> x0, blocking collectives: 26.9 us -> none  [shards(): got = lax.all_to_all(send, 'wide', split_axis=0, concat_axis=0, tiled=True)]
    dot_general x1, matrix products: 0.48 us -> 1.52 us  [shards(): return jnp.dot(amplitudes, full, preferred_element_type=jnp.float32)]
    unnamed x12 -> x8, local copies, waits for them, and re-layouts: 2.05 us -> 1.14 us
where the time goes in v2:
time: 61.2 us; the launch traced here: 61 us
  Pallas kernels  55.7 us (91%)
  local copies, waits for them, and re-layouts  2.14 us (3%)
  matrix products  1.52 us (2%)
  other arithmetic  0.81 us (1%)
  between operations  0.79 us (1%)
    pallas_call x1, Pallas kernels, shards(): pl.pallas_call(functools.partial(exchange, (x_count, y_count, own_count,...  55.7 us
    dot_general x1, matrix products, shards(): return jnp.dot(amplitudes, full, preferred_element_type=jnp.float32)  1.52 us

profile of v2, /device:TPU:8, one launch (start us, length us, event | category | flops | bytes accessed | tf_op | source)
XLA Modules:
  0.0 61.0 jit_solution(5627249732883621769)
XLA Ops:
  0.0 0.0 copy-start
  0.7 0.0 copy-start.2
  0.8 0.0 copy-start.3
  0.8 0.6 %copy-done.2 = s32[128]{0:T(128)S(1)} copy-done((s32[128]{0:T(128)S(1)}, s32[128]{0:T(128)}, u32[]{:S(2)}) %copy-start.2) | copy-done | bytes 536
  1.4 0.0 copy-done.3
  1.4 0.0 copy-start.1
  1.4 0.2 select_reduce_fusion.1
  1.6 0.5 copy-done.1
  2.1 0.6 %select_reduce_fusion.code_ref = s32[64]{0:T(128)} fusion(s32[64]{0:T(128)S(1)} %get-tuple-element.6, s32[64]{0:T(128)S(1)} %get-tuple-element.5), kind=kLoop, calls=%fused_computation.1 | loop fusion | flops 12224 | bytes 768 | tf_op jit(solution)/shard_map/reduce_sum | solution.py:163
  2.7 55.7 %shard_map.64 = bf16[8,16,8,256]{3,2,1,0:T(8,128)(2,1)} custom-call(s32[64]{0:T(128)} %select_reduce_fusion.code_ref, bf16[64,8,128]{2,1,0:T(8,128)(2,1)} %tiles_ref.1), custom_call_target="tpu_custom_call" | custom-call | tf_op jit(solution)/shard_map/pallas_call | solution.py:167
  58.5 0.0 copy-done
  58.5 1.5 %convolution_bitcast_fusion = f32[512,256]{0,1:T(8,128)S(1)} fusion(bf16[1024,256]{1,0:T(8,128)(2,1)} %bitcast.7, bf16[512,1024]{1,0:T(8,128)(2,1)S(1)} %copy-done), kind=kOutput, calls=%fused_computation | convolution fusion | flops 268435456 | bytes 2097152 | tf_op jit(solution)/shard_map/dot_general | solution.py:189
  60.0 1.0 %copy.8 = f32[512,256]{1,0:T(8,128)} copy(f32[512,256]{0,1:T(8,128)S(1)} %convolution_bitcast_fusion) | data formatting | bytes 1048576 | tf_op jit(solution)/shard_map/dot_general | solution.py:189
  (1 shorter events, 0.0 us)
Async XLA Ops:
  0.0 58.5 %copy-start = (bf16[512,1024]{1,0:T(8,128)(2,1)S(1)}, bf16[512,1024]{1,0:T(8,128)(2,1)}, u32[]{:S(2)}) copy-start(bf16[512,1024]{1,0:T(8,128)(2,1)} %param.6) | copy-start | bytes 3145732
  0.7 0.7 %copy-start.2 = (s32[128]{0:T(128)S(1)}, s32[128]{0:T(128)}, u32[]{:S(2)}) copy-start(s32[128]{0:T(128)} %param.11) | copy-start | bytes 1540
  0.8 0.7 %copy-start.3 = (s32[64]{0:T(128)S(1)}, s32[64]{0:T(128)}, u32[]{:S(2)}) copy-start(s32[64]{0:T(128)} %param.10) | copy-start | bytes 772
  1.4 0.7 %copy-start.1 = (s32[64]{0:T(128)S(1)}, s32[64]{0:T(128)}, u32[]{:S(2)}) copy-start(s32[64]{0:T(128)} %param.8) | copy-start | bytes 772

commit v3 on v1

v3 whole, which is shorter than its diff:
```python
import functools

import jax
import jax.numpy as jnp
from jax import lax
from jax.experimental import pallas as pl
from jax.experimental.pallas import tpu as pltpu
from jax.sharding import PartitionSpec as P

MESH = pl.DeviceIdType.MESH
CORES = 2
LABELS = 32
FANS = 4


def away(d, count):
    return min(d, count - d)


def exchange(
    sizes,
    tiles_hbm,
    in_hbm,
    counts_ref,
    out_hbm,
    map_hbm,
    full_ref,
    tiles_ref,
    in_ref,
    out_tile_ref,
    map_ref,
    code_vmem,
    code_ref,
    send,
    send_label,
    got,
    got_label,
    block_ref,
    load_sem,
    tile_send,
    tile_recv,
    label_send,
    label_recv,
    block_send,
    far_recv,
    near_recv,
):
    x_count, y_count, own_count, tile_count = sizes
    e_count = x_count * CORES
    wide_count = e_count * y_count
    slot_count, _, width = tiles_ref.shape
    n_count = lax.axis_size("narrow")
    wide = lax.axis_index("wide")
    me = lax.axis_index("narrow")
    core = wide % CORES
    y = (wide // CORES) % y_count
    x = wide // (CORES * y_count)

    def wide_at(dy, de):
        to_x = (x + de // CORES) % x_count
        to_y = (y + dy) % y_count
        to_core = (core + de % CORES) % CORES
        return (to_x * y_count + to_y) * CORES + to_core

    stride = n_count // FANS
    far = [stride * i for i in sorted(range(1, FANS), key=lambda i: -away(i, FANS))]
    near = [(d if away(d, stride) < stride / 2 else None) for d in range(1, stride)]
    near = [d if d is None or d < stride / 2 else d - stride for d in near]
    side = jnp.where(core == 0, stride // 2, n_count - stride // 2)

    def at(offset):
        return (me + n_count + offset) % n_count

    near = [at(side if d is None else d) for d in near]
    column = [at(d) for d in far] + near
    column += [at(-side)] if stride > 1 and stride % 2 == 0 else []
    partners = [(dy, de) for dy in range(y_count) for de in range(e_count) if (dy, de) != (0, 0)]
    partners.sort(key=lambda p: -(away(p[0], y_count) + away(p[1] // CORES, x_count)))

    loads = [
        pltpu.make_async_copy(src, dst, load_sem.at[i])
        for i, (src, dst) in enumerate(
            [
                (out_hbm, out_tile_ref),
                (map_hbm, map_ref),
                (in_hbm, in_ref),
                (tiles_hbm, tiles_ref),
            ]
        )
    ]
    for load in loads:
        load.start()
    barrier = pltpu.get_barrier_semaphore()
    for dy, de in partners:
        pl.semaphore_signal(
            barrier, inc=1, device_id={"wide": wide_at(dy, de)}, device_id_type=MESH
        )
    for n in column:
        pl.semaphore_signal(barrier, inc=1, device_id={"narrow": n}, device_id_type=MESH)
    for load in loads[:3]:
        load.wait()

    bf16, f32, i32 = jnp.bfloat16, jnp.float32, jnp.int32
    tile_total = map_ref.shape[1]
    hit = lax.broadcasted_iota(i32, (tile_total, slot_count), 0) == jnp.broadcast_to(
        out_tile_ref[...], (tile_total, slot_count)
    )
    place = jnp.dot(
        jnp.broadcast_to(map_ref[...].astype(f32), (8, tile_total)).astype(bf16),
        hit.astype(f32).astype(bf16),
        preferred_element_type=f32,
    ).astype(i32)
    slot = lax.broadcasted_iota(i32, (8, slot_count), 1)
    target = jnp.where(slot < counts_ref[0], place // own_count, -1)
    label = (place % own_count) * tile_count + in_ref[...] + 1
    kinds = jnp.where(lax.broadcasted_iota(i32, (8, slot_count), 0) == 0, slot, label)
    match = lax.broadcasted_iota(i32, (wide_count, slot_count), 0) == jnp.broadcast_to(
        target[:1], (wide_count, slot_count)
    )
    found = lax.dot_general(
        kinds.astype(f32).astype(bf16),
        match.astype(f32).astype(bf16),
        (((1,), (1,)), ((), ())),
        preferred_element_type=f32,
    ).astype(i32)
    code_vmem[...] = found[:1] * LABELS + found[1:2]
    to_scalar = pltpu.make_async_copy(code_vmem, code_ref, load_sem.at[0])
    to_scalar.start()
    loads[3].wait()
    to_scalar.wait()

    for dy, de in partners + [(0, 0)]:
        spot = dy * e_count + de
        code = code_ref[0, wide_at(dy, de)]
        rows, labels = (send, send_label) if spot else (got, got_label)
        rows[spot] = tiles_ref[jnp.clip(code // LABELS, 0, slot_count - 1)]
        labels[spot] = jnp.full((1, width), code % LABELS, i32).astype(f32)

    pl.semaphore_wait(barrier, wide_count - 1 + len(column))

    def remote(src, dst, send_sem, recv_sem, device):
        return pltpu.make_async_remote_copy(
            src_ref=src,
            dst_ref=dst,
            send_sem=send_sem,
            recv_sem=recv_sem,
            device_id=device,
            device_id_type=MESH,
        )

    half = wide_count // 2
    for dy, de in partners:
        to = {"wide": wide_at(dy, de)}
        spot = dy * e_count + de
        group = spot // half
        remote(
            send_label.at[spot], got_label.at[spot], label_send, label_recv.at[group], to
        ).start()
        remote(send.at[spot], got.at[spot], tile_send, tile_recv.at[group], to).start()

    bins = own_count * tile_count
    sums = [jnp.zeros(tiles_ref.shape[1:], f32) for _ in range(bins)]
    to = {"wide": wide_at(0, 1)}
    for group in range(2):
        first = max(group * half, 1)
        part = pl.ds(first, (group + 1) * half - first)
        remote(send.at[part], got.at[part], tile_send, tile_recv.at[group], to).wait_recv()
        remote(
            send_label.at[part], got_label.at[part], label_send, label_recv.at[group], to
        ).wait_recv()
        for spot in range(group * half, (group + 1) * half):
            tile = got[spot].astype(f32)
            mark = jnp.broadcast_to(got_label[spot], tile.shape)
            for b in range(bins):
                sums[b] = sums[b] + jnp.where(mark == float(b + 1), tile, 0.0)
    for q in range(own_count):
        for k in range(tile_count):
            block_ref[k, :, q * width : (q + 1) * width] = sums[q * tile_count + k].astype(bf16)

    def pass_on(block, n, recv_sem, to):
        remote(block, full_ref.at[:, n], block_send, recv_sem, {"narrow": to}).start()

    for i, d in enumerate(far):
        pass_on(block_ref, me, far_recv.at[i], at(d))
    for n in near:
        pass_on(block_ref, me, near_recv, n)
    own_copy = pltpu.make_async_copy(block_ref, full_ref.at[:, me], load_sem.at[0])
    own_copy.start()
    for i, d in sorted(enumerate(far), key=lambda f: away(f[1], n_count)):
        n = at(-d)
        landed = full_ref.at[:, n]
        remote(block_ref, landed, block_send, far_recv.at[i], {"narrow": at(d)}).wait_recv()
        for to in near:
            pass_on(landed, n, near_recv, to)
    own_copy.wait()
    sent = full_ref.at[:, pl.ds(0, n_count - 1)]
    if near:
        landed = full_ref.at[:, pl.ds(0, FANS * len(near))]
        remote(landed, landed, block_send, near_recv, {"narrow": column[0]}).wait_recv()
    remote(sent, sent, block_send, near_recv, {"narrow": column[0]}).wait_send()
    every = pl.ds(1, wide_count - 1)
    remote(send.at[every], got.at[every], tile_send, tile_recv.at[0], to).wait_send()
    remote(
        send_label.at[every], got_label.at[every], label_send, label_recv.at[0], to
    ).wait_send()


def multiply(a_ref, b_ref, o_hbm, o_ref, sem):
    rows = a_ref.shape[0]
    step = min(128, rows)
    copies = []
    for i in range(rows // step):
        part = pl.ds(i * step, step)
        o_ref[part, :] = jnp.dot(a_ref[part, :], b_ref[...], preferred_element_type=jnp.float32)
        copies.append(pltpu.make_async_copy(o_ref.at[part], o_hbm.at[part], sem.at[i]))
        copies[-1].start()
    for copy in copies:
        copy.wait()


def pinned(operand):
    return pltpu.with_memory_space_constraint(operand, pltpu.HBM)


def shards(x_count, y_count, amplitudes, integrals, in_tile, counts, out_tile, owner_map):
    slot_count, piece, width = integrals.shape
    row_count, deep = amplitudes.shape
    tile_total = owner_map.shape[0]
    wide_count = lax.axis_size("wide")
    narrow_count = lax.axis_size("narrow")
    tile_count = deep // (piece * narrow_count)
    own_count = tile_total // wide_count
    wide_out = own_count * width
    vmem = pltpu.VMEM
    dma = pltpu.SemaphoreType.DMA
    bf16, f32, i32 = jnp.bfloat16, jnp.float32, jnp.int32
    hbm = pl.BlockSpec(memory_space=pl.ANY)
    whole = pl.BlockSpec(memory_space=pltpu.VMEM)
    full = pl.pallas_call(
        functools.partial(exchange, (x_count, y_count, own_count, tile_count)),
        out_shape=jax.ShapeDtypeStruct((tile_count, narrow_count, piece, wide_out), bf16),
        in_specs=[hbm, hbm, pl.BlockSpec(memory_space=pltpu.SMEM), hbm, hbm],
        out_specs=hbm,
        cost_estimate=pl.CostEstimate(flops=10**9, bytes_accessed=10**8, transcendentals=0),
        scratch_shapes=[
            vmem((slot_count, piece, width), bf16),
            vmem((1, slot_count), i32),
            vmem((1, slot_count), i32),
            vmem((1, tile_total), i32),
            vmem((1, wide_count), i32),
            pltpu.SMEM((1, wide_count), i32),
            vmem((wide_count, piece, width), bf16),
            vmem((wide_count, 1, width), f32),
            vmem((wide_count, piece, width), bf16),
            vmem((wide_count, 1, width), f32),
            vmem((tile_count, piece, wide_out), bf16),
            dma((4,)),
            dma(()),
            dma((2,)),
            dma(()),
            dma((2,)),
            dma(()),
            dma((FANS - 1,)),
            dma(()),
        ],
        compiler_params=pltpu.CompilerParams(
            collective_id=0, has_side_effects=True, vmem_limit_bytes=8 << 20
        ),
    )(
        pinned(integrals),
        pinned(in_tile.reshape(1, slot_count)),
        counts,
        pinned(out_tile.reshape(1, slot_count)),
        pinned(owner_map.reshape(1, tile_total)),
    )
    full = full.reshape(deep, wide_out)
    return pl.pallas_call(
        multiply,
        out_shape=jax.ShapeDtypeStruct((row_count, wide_out), f32),
        in_specs=[whole, whole],
        out_specs=hbm,
        scratch_shapes=[vmem((row_count, wide_out), f32), dma((8,))],
        compiler_params=pltpu.CompilerParams(vmem_limit_bytes=8 << 20),
    )(amplitudes, full)


def solution(mesh):
    wide_count = mesh.shape["wide"]
    y_count = 8 if wide_count == 64 else max(1, wide_count // 4)
    x_count = wide_count // (CORES * y_count)
    return jax.shard_map(
        functools.partial(shards, x_count, y_count),
        mesh=mesh,
        in_specs=(
            P("narrow", None),
            P("wide", "narrow", None),
            P("wide"),
            P("wide"),
            P("wide"),
            P(),
        ),
        out_specs=P("narrow", "wide"),
        check_vma=False,
    )
```

time: 72.8 us -> 47.5 us (0.65)
  blocking collectives: 66.3 us -> 0 us
  Pallas kernels: 0 us -> 46.7 us
  local copies, waits for them, and re-layouts: 3.65 us -> 0.01 us
  other arithmetic: 0.98 us -> 0 us
  matrix products: 0.79 us -> 0 us
    pallas_call x0 -> x2, Pallas kernels: none -> 46.7 us  [the longest x1 45.5 us: shards(): pl.pallas_call(functools.partial(exchange, (x_count, y_count, own_count,...]
    all_gather x1 -> x0, blocking collectives: 39.5 us -> none  [shards(): full = lax.all_gather(summed, 'narrow', axis=0)]
    all_to_all x1 -> x0, blocking collectives: 26.9 us -> none  [shards(): got = lax.all_to_all(send, 'wide', split_axis=0, concat_axis=0, tiled=True)]
    unnamed x12 -> x2, local copies, waits for them, and re-layouts: 2.05 us -> 0.01 us
    dot_general x1 -> x0, local copies, waits for them, and re-layouts: 1 us -> none  [shards(): return jnp.dot(amplitudes, full, preferred_element_type=jnp.float32)]
    dot_general x3 -> x0, matrix products: 0.79 us -> none  [the longest x1 0.48 us: shards(): return jnp.dot(amplitudes, full, preferred_element_type=jnp.float32)]
where the time goes in v3:
time: 47.5 us; the launch traced here: 47.4 us
  Pallas kernels  46.7 us (98%)
  between operations  0.68 us (1%)
    pallas_call x1, Pallas kernels, shards(): pl.pallas_call(functools.partial(exchange, (x_count, y_count, own_count,...  45.5 us
    pallas_call x1, Pallas kernels, shards(): pl.pallas_call(multiply, out_shape=jax.ShapeDtypeStruct((row_count, wide_...  1.22 us

profile of v3, /device:TPU:8, one launch (start us, length us, event | category | flops | bytes accessed | tf_op | source)
XLA Modules:
  0.0 47.4 jit_solution(2833218002924500174)
XLA Ops:
  0.7 0.0 copy-start
  0.7 45.5 %shard_map.64 = bf16[8,16,8,256]{3,2,1,0:T(8,128)(2,1)S(1)} custom-call(bf16[64,8,128]{2,1,0:T(8,128)(2,1)} %tiles_hbm.1, s32[1,64]{1,0:T(1,128)} %bitcast.5, s32[1]{0:T(128)S(6)} %copy.7.counts_ref, s32[1,64]{1,0:T(1,128)} %bitcast.6, s32[1,128]{1,0:T(1,128)} %bitcast.7), custom_call_target="tpu_custom_call" | custom-call | flops 1000000000 | bytes 100000000 | tf_op jit(solution)/shard_map/pallas_call | solution.py:239
  46.2 0.0 copy-done
  46.2 1.2 %shard_map.65 = f32[512,256]{1,0:T(8,128)} custom-call(bf16[512,1024]{1,0:T(8,128)(2,1)S(1)} %copy-done, bf16[1024,256]{1,0:T(8,128)(2,1)S(1)} %bitcast.4), custom_call_target="tpu_custom_call" | custom-call | tf_op jit(solution)/shard_map/pallas_call | solution.py:277
Async XLA Ops:
  0.7 45.5 %copy-start = (bf16[512,1024]{1,0:T(8,128)(2,1)S(1)}, bf16[512,1024]{1,0:T(8,128)(2,1)}, u32[]{:S(2)}) copy-start(bf16[512,1024]{1,0:T(8,128)(2,1)} %a_ref.1) | copy-start | bytes 3145732

commit v4 on v3

--- a/solution.py
+++ b/solution.py
@@ -43,11 +43,13 @@
     label_recv,
     block_send,
     far_recv,
+    half_recv,
     near_recv,
+    plane_ready,
 ):
     x_count, y_count, own_count, tile_count = sizes
-    e_count = x_count * CORES
-    wide_count = e_count * y_count
+    chips = x_count * y_count
+    wide_count = chips * CORES
     slot_count, _, width = tiles_ref.shape
     n_count = lax.axis_size("narrow")
     wide = lax.axis_index("wide")
@@ -56,47 +58,58 @@
     y = (wide // CORES) % y_count
     x = wide // (CORES * y_count)
 
-    def wide_at(dy, de):
-        to_x = (x + de // CORES) % x_count
-        to_y = (y + dy) % y_count
-        to_core = (core + de % CORES) % CORES
+    def wide_at(j, to_core):
+        to_x = (x + j % x_count) % x_count
+        to_y = (y + j // x_count) % y_count
         return (to_x * y_count + to_y) * CORES + to_core
-
-    stride = n_count // FANS
-    far = [stride * i for i in sorted(range(1, FANS), key=lambda i: -away(i, FANS))]
-    near = [(d if away(d, stride) < stride / 2 else None) for d in range(1, stride)]
-    near = [d if d is None or d < stride / 2 else d - stride for d in near]
-    side = jnp.where(core == 0, stride // 2, n_count - stride // 2)
 
     def at(offset):
         return (me + n_count + offset) % n_count
 
-    near = [at(side if d is None else d) for d in near]
-    column = [at(d) for d in far] + near
-    column += [at(-side)] if stride > 1 and stride % 2 == 0 else []
-    partners = [(dy, de) for dy in range(y_count) for de in range(e_count) if (dy, de) != (0, 0)]
-    partners.sort(key=lambda p: -(away(p[0], y_count) + away(p[1] // CORES, x_count)))
+    stride = n_count // FANS
+    side = jnp.where(core == 0, stride // 2, -(stride // 2))
+    steps = [stride] + list(range(1, (stride + 1) // 2)) + ([side] if stride % 2 == 0 else [])
+    column = [at(sign * d) for d in steps for sign in (1, -1)]
+    near = list(range(2, 2 * len(steps)))[: stride - 1]
+    order = sorted(
+        range(chips), key=lambda j: -(away(j // x_count, y_count) + away(j % x_count, x_count))
+    )
+    others = [j for j in order if j]
+
+    def signal(sem, device):
+        pl.semaphore_signal(sem, inc=1, device_id=device, device_id_type=MESH)
+
+    def remote(src, dst, send_sem, recv_sem, device):
+        return pltpu.make_async_remote_copy(
+            src_ref=src,
+            dst_ref=dst,
+            send_sem=send_sem,
+            recv_sem=recv_sem,
+            device_id=device,
+            device_id_type=MESH,
+        )
 
     loads = [
         pltpu.make_async_copy(src, dst, load_sem.at[i])
         for i, (src, dst) in enumerate(
-            [
-                (out_hbm, out_tile_ref),
-                (map_hbm, map_ref),
-                (in_hbm, in_ref),
-                (tiles_hbm, tiles_ref),
-            ]
+            [(out_hbm, out_tile_ref), (map_hbm, map_ref), (in_hbm, in_ref), (tiles_hbm, tiles_ref)]
         )
     ]
     for load in loads:
         load.start()
+
     barrier = pltpu.get_barrier_semaphore()
-    for dy, de in partners:
-        pl.semaphore_signal(
-            barrier, inc=1, device_id={"wide": wide_at(dy, de)}, device_id_type=MESH
-        )
+    for j in order:
+        signal(barrier, {"wide": wide_at(j, 1 - core)})
+        if j:
+            signal(barrier, {"wide": wide_at(j, core)})
+
     for n in column:
-        pl.semaphore_signal(barrier, inc=1, device_id={"narrow": n}, device_id_type=MESH)
+
+        @pl.when(n > me)
+        def _(n=n):
+            signal(barrier, {"narrow": n})
+
     for load in loads[:3]:
         load.wait()
 
@@ -129,79 +142,104 @@
     loads[3].wait()
     to_scalar.wait()
 
-    for dy, de in partners + [(0, 0)]:
-        spot = dy * e_count + de
-        code = code_ref[0, wide_at(dy, de)]
-        rows, labels = (send, send_label) if spot else (got, got_label)
+    def gather(j, to_core, rows, labels, spot):
+        code = code_ref[0, wide_at(j, to_core)]
         rows[spot] = tiles_ref[jnp.clip(code // LABELS, 0, slot_count - 1)]
         labels[spot] = jnp.full((1, width), code % LABELS, i32).astype(f32)
 
-    pl.semaphore_wait(barrier, wide_count - 1 + len(column))
-
-    def remote(src, dst, send_sem, recv_sem, device):
-        return pltpu.make_async_remote_copy(
-            src_ref=src,
-            dst_ref=dst,
-            send_sem=send_sem,
-            recv_sem=recv_sem,
-            device_id=device,
-            device_id_type=MESH,
-        )
-
-    half = wide_count // 2
-    for dy, de in partners:
-        to = {"wide": wide_at(dy, de)}
-        spot = dy * e_count + de
-        group = spot // half
+    for to_core in range(CORES):
+        for j in order:
+            gather(j, to_core, send, send_label, to_core * chips + j)
+    gather(0, core, got, got_label, core * chips)
+
+    lower = sum(jnp.where(n < me, 1, 0) for n in column)
+    pl.semaphore_wait(barrier, wide_count - 1 + lower)
+
+    def send_to(j, to_core):
+        device = {"wide": wide_at(j, to_core)}
+        out, spot, other = to_core * chips + j, core * chips + j, (core + to_core) % CORES
         remote(
-            send_label.at[spot], got_label.at[spot], label_send, label_recv.at[group], to
+            send_label.at[out], got_label.at[spot], label_send, label_recv.at[other], device
         ).start()
-        remote(send.at[spot], got.at[spot], tile_send, tile_recv.at[group], to).start()
+        remote(send.at[out], got.at[spot], tile_send, tile_recv.at[other], device).start()
+
+    for j in others:
+        for to_core in range(CORES):
+            send_to(j, to_core)
+    send_to(0, 1 - core)
+
+    for i, n in enumerate(column):
+
+        @pl.when(n < me)
+        def _(i=i, n=n):
+            signal(plane_ready.at[i ^ 1], {"narrow": n})
 
     bins = own_count * tile_count
     sums = [jnp.zeros(tiles_ref.shape[1:], f32) for _ in range(bins)]
-    to = {"wide": wide_at(0, 1)}
-    for group in range(2):
-        first = max(group * half, 1)
-        part = pl.ds(first, (group + 1) * half - first)
-        remote(send.at[part], got.at[part], tile_send, tile_recv.at[group], to).wait_recv()
+    mate = {"wide": wide_at(0, 1 - core)}
+    for other in range(CORES):
+        base = (core if other == 0 else 1 - core) * chips
+        part = pl.ds(base + 1, chips - 1) if other == 0 else pl.ds(base, chips)
+        remote(got.at[part], got.at[part], tile_send, tile_recv.at[other], mate).wait_recv()
         remote(
-            send_label.at[part], got_label.at[part], label_send, label_recv.at[group], to
+            got_label.at[part], got_label.at[part], label_send, label_recv.at[other], mate
         ).wait_recv()
-        for spot in range(group * half, (group + 1) * half):
-            tile = got[spot].astype(f32)
-            mark = jnp.broadcast_to(got_label[spot], tile.shape)
+        for j in range(chips):
+            tile = got[base + j].astype(f32)
+            mark = jnp.broadcast_to(got_label[base + j], tile.shape)
             for b in range(bins):
                 sums[b] = sums[b] + jnp.where(mark == float(b + 1), tile, 0.0)
     for q in range(own_count):
         for k in range(tile_count):
             block_ref[k, :, q * width : (q + 1) * width] = sums[q * tile_count + k].astype(bf16)
 
-    def pass_on(block, n, recv_sem, to):
-        remote(block, full_ref.at[:, n], block_send, recv_sem, {"narrow": to}).start()
-
-    for i, d in enumerate(far):
-        pass_on(block_ref, me, far_recv.at[i], at(d))
-    for n in near:
-        pass_on(block_ref, me, near_recv, n)
-    own_copy = pltpu.make_async_copy(block_ref, full_ref.at[:, me], load_sem.at[0])
+    def pass_on(src, dst, recv_sem, n):
+        remote(src, dst, block_send, recv_sem, {"narrow": n}).start()
+
+    def wait_ready(i, n):
+        @pl.when(n > me)
+        def _():
+            pl.semaphore_wait(plane_ready.at[i], 1)
+
+    mine = full_ref.at[:, me]
+    first = jnp.where(column[0] < n_count // 2, 0, 1)
+    sides = [
+        (i, jnp.where(i == 0, column[0], column[1]), jnp.where(i == 0, column[1], column[0]))
+        for i in (first, 1 - first)
+    ]
+    for i, n, _ in sides:
+        wait_ready(i, n)
+        pass_on(block_ref, mine, far_recv.at[1 - i], n)
+    for i in near:
+        wait_ready(i, column[i])
+        pass_on(block_ref, mine, near_recv, column[i])
+    for i in range(2 + len(near), len(column)):
+        wait_ready(i, column[i])
+    own_copy = pltpu.make_async_copy(block_ref, mine, load_sem.at[0])
     own_copy.start()
-    for i, d in sorted(enumerate(far), key=lambda f: away(f[1], n_count)):
-        n = at(-d)
+    size = tile_count // 2
+    for i, n, beyond in sides:
         landed = full_ref.at[:, n]
-        remote(block_ref, landed, block_send, far_recv.at[i], {"narrow": at(d)}).wait_recv()
+        remote(landed, landed, block_send, far_recv.at[i], {"narrow": n}).wait_recv()
+        half = full_ref.at[pl.ds((1 - i) * size, size), n]
+        pass_on(half, half, half_recv.at[i], beyond)
         for to in near:
-            pass_on(landed, n, near_recv, to)
+            pass_on(landed, landed, near_recv, column[to])
+    for i, n, _ in sides:
+        half = full_ref.at[pl.ds((1 - i) * size, size), at(n_count // 2)]
+        remote(half, half, block_send, half_recv.at[i], {"narrow": n}).wait_recv()
+        for to in near:
+            pass_on(half, half, near_recv, column[to])
     own_copy.wait()
-    sent = full_ref.at[:, pl.ds(0, n_count - 1)]
     if near:
         landed = full_ref.at[:, pl.ds(0, FANS * len(near))]
         remote(landed, landed, block_send, near_recv, {"narrow": column[0]}).wait_recv()
+    sent = full_ref.at[:, pl.ds(0, n_count - 1)]
     remote(sent, sent, block_send, near_recv, {"narrow": column[0]}).wait_send()
     every = pl.ds(1, wide_count - 1)
-    remote(send.at[every], got.at[every], tile_send, tile_recv.at[0], to).wait_send()
+    remote(send.at[every], got.at[every], tile_send, tile_recv.at[0], mate).wait_send()
     remote(
-        send_label.at[every], got_label.at[every], label_send, label_recv.at[0], to
+        send_label.at[every], got_label.at[every], label_send, label_recv.at[0], mate
     ).wait_send()
 
 
@@ -260,8 +298,10 @@
             dma(()),
             dma((2,)),
             dma(()),
-            dma((FANS - 1,)),
+            dma((2,)),
+            dma((2,)),
             dma(()),
+            pltpu.SemaphoreType.REGULAR((narrow_count,)),
         ],
         compiler_params=pltpu.CompilerParams(
             collective_id=0, has_side_effects=True, vmem_limit_bytes=8 << 20

time: 47.5 us -> 45.1 us (0.949)
  Pallas kernels: 46.7 us -> 44.3 us
    pallas_call x1, Pallas kernels: 45.5 us -> 43 us  [shards(): pl.pallas_call(functools.partial(exchange, (x_count, y_count, own_count,...]
where the time goes in v4:
time: 45.1 us; the launch traced here: 44.9 us
  Pallas kernels  44.3 us (98%)
  between operations  0.68 us (2%)
    pallas_call x1, Pallas kernels, shards(): pl.pallas_call(functools.partial(exchange, (x_count, y_count, own_count,...  43 us
    pallas_call x1, Pallas kernels, shards(): pl.pallas_call(multiply, out_shape=jax.ShapeDtypeStruct((row_count, wide_...  1.22 us

profile of v4, /device:TPU:8, one launch (start us, length us, event | category | flops | bytes accessed | tf_op | source)
XLA Modules:
  0.0 44.9 jit_solution(4477693772171175704)
XLA Ops:
  0.7 0.0 copy-start
  0.7 43.0 %shard_map.64 = bf16[8,16,8,256]{3,2,1,0:T(8,128)(2,1)S(1)} custom-call(bf16[64,8,128]{2,1,0:T(8,128)(2,1)} %tiles_hbm.1, s32[1,64]{1,0:T(1,128)} %bitcast.5, s32[1]{0:T(128)S(6)} %copy.7.counts_ref, s32[1,64]{1,0:T(1,128)} %bitcast.6, s32[1,128]{1,0:T(1,128)} %bitcast.7), custom_call_target="tpu_custom_call" | custom-call | flops 1000000000 | bytes 100000000 | tf_op jit(solution)/shard_map/pallas_call | solution.py:277
  43.7 0.0 copy-done
  43.7 1.2 %shard_map.65 = f32[512,256]{1,0:T(8,128)} custom-call(bf16[512,1024]{1,0:T(8,128)(2,1)S(1)} %copy-done, bf16[1024,256]{1,0:T(8,128)(2,1)S(1)} %bitcast.4), custom_call_target="tpu_custom_call" | custom-call | tf_op jit(solution)/shard_map/pallas_call | solution.py:317
Async XLA Ops:
  0.7 43.1 %copy-start = (bf16[512,1024]{1,0:T(8,128)(2,1)S(1)}, bf16[512,1024]{1,0:T(8,128)(2,1)}, u32[]{:S(2)}) copy-start(bf16[512,1024]{1,0:T(8,128)(2,1)} %a_ref.1) | copy-start | bytes 3145732

commit v5 on v4

--- a/solution.py
+++ b/solution.py
@@ -155,18 +155,15 @@
     lower = sum(jnp.where(n < me, 1, 0) for n in column)
     pl.semaphore_wait(barrier, wide_count - 1 + lower)
 
-    def send_to(j, to_core):
-        device = {"wide": wide_at(j, to_core)}
-        out, spot, other = to_core * chips + j, core * chips + j, (core + to_core) % CORES
-        remote(
-            send_label.at[out], got_label.at[spot], label_send, label_recv.at[other], device
-        ).start()
-        remote(send.at[out], got.at[spot], tile_send, tile_recv.at[other], device).start()
-
-    for j in others:
-        for to_core in range(CORES):
-            send_to(j, to_core)
-    send_to(0, 1 - core)
+    targets = [(j, to_core) for j in others for to_core in range(CORES)] + [(0, 1 - core)]
+    for src, dst, s_sem, r_sem in (
+        (send, got, tile_send, tile_recv),
+        (send_label, got_label, label_send, label_recv),
+    ):
+        for j, to_core in targets:
+            out, spot, other = to_core * chips + j, core * chips + j, (core + to_core) % CORES
+            device = {"wide": wide_at(j, to_core)}
+            remote(src.at[out], dst.at[spot], s_sem, r_sem.at[other], device).start()
 
     for i, n in enumerate(column):
 
@@ -245,7 +242,7 @@
 
 def multiply(a_ref, b_ref, o_hbm, o_ref, sem):
     rows = a_ref.shape[0]
-    step = min(128, rows)
+    step = min(64, rows)
     copies = []
     for i in range(rows // step):
         part = pl.ds(i * step, step)

time: 45.1 us -> 45.7 us (1.013)
  Pallas kernels: 44.3 us -> 44.9 us
where the time goes in v5:
time: 45.7 us; the launch traced here: 45.5 us
  Pallas kernels  44.9 us (98%)
  between operations  0.68 us (1%)
    pallas_call x1, Pallas kernels, shards(): pl.pallas_call(functools.partial(exchange, (x_count, y_count, own_count,...  43.3 us
    pallas_call x1, Pallas kernels, shards(): pl.pallas_call(multiply, out_shape=jax.ShapeDtypeStruct((row_count, wide_...  1.56 us

profile of v5, /device:TPU:8, one launch (start us, length us, event | category | flops | bytes accessed | tf_op | source)
XLA Modules:
  0.0 45.5 jit_solution(15834232397596938343)
XLA Ops:
  0.7 0.0 copy-start
  0.7 43.3 %shard_map.64 = bf16[8,16,8,256]{3,2,1,0:T(8,128)(2,1)S(1)} custom-call(bf16[64,8,128]{2,1,0:T(8,128)(2,1)} %tiles_hbm.1, s32[1,64]{1,0:T(1,128)} %bitcast.5, s32[1]{0:T(128)S(6)} %copy.7.counts_ref, s32[1,64]{1,0:T(1,128)} %bitcast.6, s32[1,128]{1,0:T(1,128)} %bitcast.7), custom_call_target="tpu_custom_call" | custom-call | flops 1000000000 | bytes 100000000 | tf_op jit(solution)/shard_map/pallas_call | solution.py:274
  44.0 0.0 copy-done
  44.0 1.6 %shard_map.65 = f32[512,256]{1,0:T(8,128)} custom-call(bf16[512,1024]{1,0:T(8,128)(2,1)S(1)} %copy-done, bf16[1024,256]{1,0:T(8,128)(2,1)S(1)} %bitcast.4), custom_call_target="tpu_custom_call" | custom-call | tf_op jit(solution)/shard_map/pallas_call | solution.py:314
Async XLA Ops:
  0.7 43.3 %copy-start = (bf16[512,1024]{1,0:T(8,128)(2,1)S(1)}, bf16[512,1024]{1,0:T(8,128)(2,1)}, u32[]{:S(2)}) copy-start(bf16[512,1024]{1,0:T(8,128)(2,1)} %a_ref.1) | copy-start | bytes 3145732
